TPU v7x, 512 devices: a whole 4x4x16 slice. The times are simulated.
512 devices in a mesh: row: 64 (over z_hi, x, y), col: 8 (over z_lo, core).
Axes of the slice: x: 4, y: 4, z: 16 (z_hi: 4, z_lo: 4; z = z_hi * 4 + z_lo), core: 2. Of those that a mesh axis runs over, the one named last changes fastest.
Arguments:
- tensor: float32 [8, 8192, 8192], P(None, 'row', 'col'), may hold values from -0.8 to 0.8
- factor_a: float32 [8192, 256], P(('row', 'col')), may hold values from -0.0625 to 0.0625
- factor_bt: float32 [256, 8192], P('row', 'col'), may hold values from -0.0625 to 0.0625
- factor_c: float32 [8, 256], replicated, may hold values from -6 to 6
Outputs:
- grad_a: float32 [8192, 256], P(('row', 'col'))
- grad_bt: float32 [256, 8192], P('row', 'col')
- grad_c: float32 [8, 256], replicated
All inputs are finite; a program needn't handle non-finite values.
Results may differ from a plain program's by a relative error of at most 0.0001.
Values sent between devices are 32-bit elements; how exact they have to be, the bound alone decides.
A program may use at most 64 MiB of HBM per device.

v0:
```python
import jax
import jax.numpy as jnp
from jax import lax
from jax.sharding import PartitionSpec as P


def local(tensor, factor_a, factor_bt, factor_c):
    highest = lax.Precision.HIGHEST
    rank_rows = factor_bt.shape[0]
    block_a = lax.all_gather(factor_a, "col", axis=0, tiled=True)
    gram_c = jnp.dot(factor_c.T, factor_c, precision=highest)
    weighted = block_a[None, :, :] * factor_c[:, None, :]
    block_bt = lax.all_gather(factor_bt, "row", axis=0, tiled=True)
    mttkrp_bt = lax.psum_scatter(
        jnp.einsum("kir,kij->rj", weighted, tensor, precision=highest),
        "row",
        scatter_dimension=0,
        tiled=True,
    )
    contracted = jnp.einsum("kij,rj->kir", tensor, block_bt, precision=highest)
    partial_a = jnp.sum(contracted * factor_c[:, None, :], axis=0)
    partial_c = jnp.sum(contracted * block_a[None, :, :], axis=1)
    mttkrp_a = lax.psum_scatter(partial_a, "col", scatter_dimension=0, tiled=True)
    mttkrp_c = lax.psum(partial_c, ("row", "col"))
    local_gram_a = jnp.dot(factor_a.T, factor_a, precision=highest)
    gram_a = lax.psum(local_gram_a, ("row", "col"))
    gram_b = lax.psum(jnp.dot(block_bt, block_bt.T, precision=highest), "col")
    grad_a = jnp.dot(factor_a, gram_b * gram_c, precision=highest) - mttkrp_a
    h_rows = lax.dynamic_slice_in_dim(
        gram_a * gram_c, lax.axis_index("row") * rank_rows, rank_rows, 0
    )
    grad_bt = jnp.dot(h_rows, block_bt, precision=highest) - mttkrp_bt
    grad_c = jnp.dot(factor_c, gram_a * gram_b, precision=highest) - mttkrp_c
    return (grad_a, grad_bt, grad_c)


def solution(mesh):
    in_specs = (P(None, "row", "col"), P(("row", "col"), None), P("row", "col"), P())
    out_specs = (P(("row", "col"), None), P("row", "col"), P())
    return jax.shard_map(local, mesh=mesh, in_specs=in_specs, out_specs=out_specs, check_vma=False)
```

profile of v0, /device:TPU:2, one launch (start us, length us, event | category | flops | bytes accessed | tf_op | source)
XLA Modules:
  0.0 1439.3 jit_solution(11810171701839936095)
XLA Ops:
  8.0 0.0 all-gather.3.cloned.1.call-start
  8.0 0.7 all-gather.3.cloned.1.call-update
  8.7 0.0 all-reduce.7.cloned.1.call-start
  8.8 1.9 fusion.11
  10.7 0.0 all-reduce.7.cloned.1.call-update
  10.7 0.0 all-reduce.9.cloned.1.call-start
  10.8 15.1 %all_gather.7 = f32[128,256]{1,0:T(8,128)S(1)} all-gather(f32[16,256]{1,0:T(8,128)} %param.5), channel_id=1, replica_groups=mesh['row'=64,'col'=8] {'col'}, dimensions={0}, use_global_device_ids=true | all-gather | bytes 147456 | tf_op jit(solution)/shard_map/all_gather | solution.py:10
  25.9 0.0 copy-start.2
  25.9 6.8 convolution_bitcast_fusion
  32.7 0.0 all-reduce.9.cloned.1.call-update
  32.7 0.0 reduce-scatter.2.cloned.1.call-start
  32.7 89.5 %all-gather.3.cloned.1.call-done = f32[64,4,1024]{2,1,0:T(4,128)} async-done(((f32[1,4,1024]{2,1,0:T(4,128)}), f32[64,4,1024]{2,1,0:T(4,128)}) %all-gather.3.cloned.1.call-update) | async-done | bytes 1048592 | tf_op jit(solution)/shard_map/all_gather | solution.py:13
  122.3 0.0 copy-start
  122.3 1.7 reshape.10
  123.9 0.0 copy-done.2
  124.0 6.3 multiply_reduce_fusion
  130.3 0.0 reduce-scatter.2.cloned.1.call-update
  130.3 0.0 all-reduce.5.cloned.1.call-start
  130.3 0.0 copy-done
  130.4 0.4 reshape.9
  130.7 1.7 fusion.9
  132.5 0.0 all-reduce.5.cloned.1.call-update
  132.5 0.4 fusion.10
  132.9 1.3 dynamic-slice
  134.9 100.0 %psum.23 = f32[8,256]{1,0:T(8,128)S(1)} all-reduce(f32[8,256]{1,0:T(8,128)S(1)} %get-tuple-element.3), channel_id=1, replica_groups=mesh['row'=64,'col'=8] {'row','col'}, use_global_device_ids=true, to_apply=%region_6.0 | all-reduce | flops 2048 | bytes 16384 | tf_op jit(solution)/shard_map/psum | solution.py:24
  234.8 257.2 %all-reduce.7.cloned.1.call-done = f32[256,256]{1,0:T(8,128)} async-done(((f32[256,256]{1,0:T(8,128)}), f32[256,256]{1,0:T(8,128)}) %all-reduce.7.cloned.1.call-update) | async-done | bytes 262160 | tf_op jit(solution)/shard_map/psum | solution.py:26
  492.0 845.5 %all-reduce.9.cloned.1.call-done = f32[256,1024]{1,0:T(8,128)} async-done(((f32[256,1024]{1,0:T(8,128)}), f32[256,1024]{1,0:T(8,128)}) %all-reduce.9.cloned.1.call-update) | async-done | bytes 1048592
  1337.5 2.0 convolution_subtract_fusion
  1339.5 88.5 %all-reduce.5.cloned.1.call-done = f32[256,256]{1,0:T(8,128)} async-done(((f32[256,256]{1,0:T(8,128)}), f32[256,256]{1,0:T(8,128)}) %all-reduce.5.cloned.1.call-update) | async-done | bytes 262160 | tf_op jit(solution)/shard_map/psum | solution.py:27
  1428.0 0.0 copy-done.1
  1428.0 1.8 fusion
  1429.9 1.9 fusion.1
  (2 shorter events, 0.0 us)
Async XLA Ops:
  8.0 114.3 %all-gather.3.cloned.1.call-start = ((), (), s32[]{:S(2)}) async-start(), calls=%async_computation.4 | async-start | bytes 1064960 | tf_op jit(solution)/shard_map/all_gather | solution.py:13
  8.7 483.3 %all-reduce.7.cloned.1.call-start = ((), (), s32[]{:S(2)}) async-start(), calls=%async_computation.3 | async-start | bytes 524288 | tf_op jit(solution)/shard_map/psum | solution.py:26
  10.7 1326.8 %all-reduce.9.cloned.1.call-start = ((), (), s32[]{:S(2)}) async-start(), calls=%async_computation.5 | async-start | bytes 2097152
  25.9 98.1 %copy-start.2 = (f32[8,256]{1,0:T(8,128)S(1)}, f32[8,256]{1,0:T(8,128)}, u32[]{:S(2)}) copy-start(f32[8,256]{1,0:T(8,128)} %param.7) | copy-start | bytes 24580
  32.7 1306.8 %reduce-scatter.2.cloned.1.call-start = ((), (), s32[]{:S(2)}) async-start(), calls=%async_computation.2 | async-start | bytes 147456 | tf_op jit(solution)/shard_map/reduce_scatter | solution.py:23
  122.3 8.1 copy-start
  130.3 1297.8 %copy-start.1 = (f32[16,256]{1,0:T(8,128)S(1)}, f32[16,256]{1,0:T(8,128)}, u32[]{:S(2)}) copy-start(f32[16,256]{1,0:T(8,128)} %param.5) | copy-start | bytes 49156
  130.3 1297.7 %all-reduce.5.cloned.1.call-start = ((), (), s32[]{:S(2)}) async-start(), calls=%async_computation.1 | async-start | bytes 524288 | tf_op jit(solution)/shard_map/psum | solution.py:27
Sparse Core Ops, SparseCore 0:
  13.0 109.2 all-gather.2
  130.4 35.3 reduce-scatter.1
Sparse Core Ops, SparseCore 1:
  14.7 477.3 all-reduce.6
  494.8 842.7 all-reduce.8
  1340.3 87.7 all-reduce.4
where the time goes:
time: 1440 us
  waiting for transfers between devices  1280 us (89%)
  blocking collectives  115 us (8%)
  matrix products  22.9 us (2%)
  between operations  16.4 us (1%)
    unnamed x6, waiting for transfers between devices  846 us
    psum x1, waiting for transfers between devices, local(): gram_a = lax.psum(local_gram_a, ('row', 'col'))  257 us
    psum x1, blocking collectives, local(): mttkrp_c = lax.psum(partial_c, ('row', 'col'))  100 us
    all_gather x1, waiting for transfers between devices, local(): block_bt = lax.all_gather(factor_bt, 'row', axis=0, tiled=True)  89.5 us
    psum x1, waiting for transfers between devices, local(): gram_b = lax.psum(jnp.dot(block_bt, block_bt.T, precision=highest), 'col')  88.5 us
  transfers between devices with their start and end apart: 5, of which 4 were waited for; matrix products, arithmetic and copies ran while one was open for 2% of the time, Pallas kernels for 0%

commit v1 on v0

--- a/solution.py
+++ b/solution.py
@@ -2,6 +2,12 @@
 import jax.numpy as jnp
 from jax import lax
 from jax.sharding import PartitionSpec as P
+
+
+def post_ratios(values):
+    everything = lax.psum(values, "col")
+    s_next = lax.psum(everything, "row")
+    return s_next
 
 
 def local(tensor, factor_a, factor_bt, factor_c):
@@ -23,7 +29,7 @@
     mttkrp_a = lax.psum_scatter(partial_a, "col", scatter_dimension=0, tiled=True)
     mttkrp_c = lax.psum(partial_c, ("row", "col"))
     local_gram_a = jnp.dot(factor_a.T, factor_a, precision=highest)
-    gram_a = lax.psum(local_gram_a, ("row", "col"))
+    gram_a = post_ratios(local_gram_a)
     gram_b = lax.psum(jnp.dot(block_bt, block_bt.T, precision=highest), "col")
     grad_a = jnp.dot(factor_a, gram_b * gram_c, precision=highest) - mttkrp_a
     h_rows = lax.dynamic_slice_in_dim(

time: 1440 us -> 1100 us (0.76)
  the two profiles are of different devices: /device:TPU:2 before, /device:TPU:16 now
where the time goes in v1:
time: 1100 us
  waiting for transfers between devices  938 us (85%)
  blocking collectives  118 us (11%)
  matrix products  22.8 us (2%)
  between operations  14.5 us (1%)
    unnamed x5, waiting for transfers between devices  778 us
    all_gather x1, waiting for transfers between devices, local(): block_bt = lax.all_gather(factor_bt, 'row', axis=0, tiled=True)  111 us
    psum x1, blocking collectives, local(): mttkrp_c = lax.psum(partial_c, ('row', 'col'))  104 us
    psum x1, waiting for transfers between devices, local(): gram_b = lax.psum(jnp.dot(block_bt, block_bt.T, precision=highest), 'col')  49.4 us
  transfers between devices with their start and end apart: 4, of which 3 were waited for; matrix products, arithmetic and copies ran while one was open for 2% of the time, Pallas kernels for 0%

profile of v1, /device:TPU:16, one launch (start us, length us, event | category | flops | bytes accessed | tf_op | source)
XLA Modules:
  0.0 1097.1 jit_solution(5120578974710595323)
XLA Ops:
  7.2 0.0 copy-start.1
  7.2 0.0 copy-start.2
  7.2 0.0 all-gather.3.cloned.1.call-start
  7.2 0.7 all-gather.3.cloned.1.call-update
  7.9 0.0 all-reduce.8.cloned.1.call-start
  8.0 1.9 fusion.11
  9.9 111.2 %all-gather.3.cloned.1.call-done = f32[64,4,1024]{2,1,0:T(4,128)} async-done(((f32[1,4,1024]{2,1,0:T(4,128)}), f32[64,4,1024]{2,1,0:T(4,128)}) %all-gather.3.cloned.1.call-update) | async-done | bytes 1048592 | tf_op jit(solution)/shard_map/all_gather | solution.py:19
  121.1 0.0 copy-start
  121.1 1.7 reshape.9
  122.8 1.7 fusion.9
  124.5 0.0 all-reduce.8.cloned.1.call-update
  124.5 0.0 reduce-scatter.2.cloned.1.call-start
  124.6 0.0 copy-done.1
  124.6 14.0 %all_gather.7 = f32[128,256]{1,0:T(8,128)S(1)} all-gather(f32[16,256]{1,0:T(8,128)S(1)} %copy-done.1), channel_id=1, replica_groups=mesh['row'=64,'col'=8] {'col'}, dimensions={0}, use_global_device_ids=true | all-gather | bytes 147456 | tf_op jit(solution)/shard_map/all_gather | solution.py:16
  138.6 0.0 copy-done
  138.6 0.4 reshape.10
  138.9 0.0 copy-done.2
  138.9 6.3 multiply_reduce_fusion
  145.3 0.0 reduce-scatter.2.cloned.1.call-update
  145.3 0.0 all-reduce.6.cloned.1.call-start
  145.3 6.7 convolution_bitcast_fusion
  152.0 49.4 %all-reduce.8.cloned.1.call-done = (f32[256,256]{1,0:T(8,128)}, f32[256,256]{1,0:T(8,128)}) async-done(((f32[256,256]{1,0:T(8,128)}, f32[256,256]{1,0:T(8,128)}), (f32[256,256]{1,0:T(8,128)}, f32[256,256]{1,0:T(8,128)})) %all-reduce.8.cloned.1.call-update) | async-done | bytes 524304 | tf_op jit(solution)/shard_map/psum | solution.py:33
  201.4 0.0 all-reduce.6.cloned.1.call-update
  201.5 1.3 dynamic-slice
  203.4 0.4 fusion.10
  203.8 104.3 %psum.31 = f32[8,256]{1,0:T(8,128)S(1)} all-reduce(f32[8,256]{1,0:T(8,128)S(1)} %get-tuple-element.3), channel_id=1, replica_groups=mesh['row'=64,'col'=8] {'row','col'}, use_global_device_ids=true, to_apply=%region_7.0 | all-reduce | flops 2048 | bytes 16384 | tf_op jit(solution)/shard_map/psum | solution.py:30
  308.1 0.0 reduce-scatter.2.cloned.1.call-done
  308.1 1.8 fusion
  309.9 776.8 %all-reduce.6.cloned.1.call-done = (f32[256,1024]{1,0:T(8,128)}, f32[256,256]{1,0:T(8,128)}) async-done(((f32[256,1024]{1,0:T(8,128)}, f32[256,256]{1,0:T(8,128)}), (f32[256,1024]{1,0:T(8,128)}, f32[256,256]{1,0:T(8,128)})) %all-reduce.6.cloned.1.call-update) | async-done | bytes 1310736
  1086.7 1.9 fusion.1
  1088.6 2.0 convolution_subtract_fusion
Async XLA Ops:
  7.2 117.4 %copy-start.1 = (f32[16,256]{1,0:T(8,128)S(1)}, f32[16,256]{1,0:T(8,128)}, u32[]{:S(2)}) copy-start(f32[16,256]{1,0:T(8,128)} %param.5) | copy-start | bytes 49156
  7.2 131.7 %copy-start.2 = (f32[8,256]{1,0:T(8,128)S(1)}, f32[8,256]{1,0:T(8,128)}, u32[]{:S(2)}) copy-start(f32[8,256]{1,0:T(8,128)} %param.7) | copy-start | bytes 24580
  7.2 113.9 %all-gather.3.cloned.1.call-start = ((), (), s32[]{:S(2)}) async-start(), calls=%async_computation.2 | async-start | bytes 1064960 | tf_op jit(solution)/shard_map/all_gather | solution.py:19
  7.9 193.5 %all-reduce.8.cloned.1.call-start = ((), (), s32[]{:S(2)}) async-start(), calls=%async_computation.4 | async-start | bytes 1048576 | tf_op jit(solution)/shard_map/psum | solution.py:33
  121.1 17.5 %copy-start = (f32[64,4,1024]{2,1,0:T(4,128)S(1)}, f32[64,4,1024]{2,1,0:T(4,128)}, u32[]{:S(2)}) copy-start(f32[64,4,1024]{2,1,0:T(4,128)} %all-gather.3.cloned.1.call-done) | copy-start | bytes 3145732
  124.5 183.6 %reduce-scatter.2.cloned.1.call-start = ((), (), s32[]{:S(2)}) async-start(), calls=%async_computation.1 | async-start | bytes 147456 | tf_op jit(solution)/shard_map/reduce_scatter | solution.py:29
  145.3 941.4 %all-reduce.6.cloned.1.call-start = ((), (), s32[]{:S(2)}) async-start(), calls=%async_computation.3 | async-start | bytes 2621440
Sparse Core Ops, SparseCore 0:
  12.2 108.8 all-gather.2
  124.7 76.7 all-reduce.7
  204.2 40.2 reduce-scatter.1
  247.3 839.3 all-reduce.5

commit v2 on v0

--- a/solution.py
+++ b/solution.py
@@ -10,7 +10,8 @@
     block_a = lax.all_gather(factor_a, "col", axis=0, tiled=True)
     gram_c = jnp.dot(factor_c.T, factor_c, precision=highest)
     weighted = block_a[None, :, :] * factor_c[:, None, :]
-    block_bt = lax.all_gather(factor_bt, "row", axis=0, tiled=True)
+    stack = jnp.stack([factor_bt] * lax.axis_size("row"))
+    block_bt = jnp.concatenate(lax.all_to_all(stack, "row", 0, 0), axis=0)
     mttkrp_bt = lax.psum_scatter(
         jnp.einsum("kir,kij->rj", weighted, tensor, precision=highest),
         "row",

time: 1440 us -> 1460 us (1.014)
  blocking collectives: 115 us -> 158 us
  waiting for transfers between devices: 1280 us -> 1240 us
  starting transfers between devices: 0.21 us -> 21.4 us
    all_gather x1 -> x0, waiting for transfers between devices: 89.5 us -> none  [local(): block_bt = lax.all_gather(factor_bt, 'row', axis=0, tiled=True)]
    psum x1, waiting for transfers between devices: 257 us -> 302 us  [local(): gram_a = lax.psum(local_gram_a, ('row', 'col'))]
    all_gather x1, blocking collectives: 15.1 us -> 51.7 us  [local(): block_a = lax.all_gather(factor_a, 'col', axis=0, tiled=True)]
    all_to_all x0 -> x1, starting transfers between devices: none -> 21.3 us  [local(): block_bt = jnp.concatenate(lax.all_to_all(stack, 'row', 0, 0), axis=0)]
    unnamed x6 -> x5, waiting for transfers between devices: 846 us -> 846 us
  transfers between devices with their start and end apart: 5 -> 5, of which waited for: 4 -> 3; matrix products, arithmetic and copies ran while one was open for 2% -> 1% of each run, Pallas kernels for 0% -> 0%
where the time goes in v2:
time: 1460 us
  waiting for transfers between devices  1240 us (85%)
  blocking collectives  158 us (11%)
  matrix products  22.9 us (2%)
  starting transfers between devices  21.4 us (1%)
  between operations  15.9 us (1%)
    unnamed x5, waiting for transfers between devices  846 us
    psum x1, waiting for transfers between devices, local(): gram_a = lax.psum(local_gram_a, ('row', 'col'))  302 us
    psum x1, blocking collectives, local(): mttkrp_c = lax.psum(partial_c, ('row', 'col'))  106 us
    psum x1, waiting for transfers between devices, local(): gram_b = lax.psum(jnp.dot(block_bt, block_bt.T, precision=highest), 'col')  88.9 us
    all_gather x1, blocking collectives, local(): block_a = lax.all_gather(factor_a, 'col', axis=0, tiled=True)  51.7 us
  transfers between devices with their start and end apart: 5, of which 3 were waited for; matrix products, arithmetic and copies ran while one was open for 1% of the time, Pallas kernels for 0%

profile of v2, /device:TPU:2, one launch (start us, length us, event | category | flops | bytes accessed | tf_op | source)
XLA Modules:
  0.0 1459.2 jit_solution(17608364075125364624)
XLA Ops:
  8.0 2.0 stack.2
  10.0 21.3 %all-to-all-start = ((f32[64,4,1024]{2,1,0:T(4,128)}), f32[64,4,1024]{2,1,0:T(4,128)S(1)}, u32[]{:S(2)}, u32[]{:S(2)}) async-start(f32[64,4,1024]{2,1,0:T(4,128)} %stack.2), calls=%async_computation | async-start | bytes 2097152 | tf_op jit(solution)/shard_map/all_to_all | solution.py:14
  31.2 0.0 all-reduce.7.cloned.1.call-start
  31.3 1.9 fusion.11
  33.2 0.0 all-reduce.7.cloned.1.call-update
  33.2 0.0 all-reduce.9.cloned.1.call-start
  33.3 51.7 %all_gather.3 = f32[128,256]{1,0:T(8,128)S(1)} all-gather(f32[16,256]{1,0:T(8,128)} %param.5), channel_id=1, replica_groups=mesh['row'=64,'col'=8] {'col'}, dimensions={0}, use_global_device_ids=true | all-gather | bytes 147456 | tf_op jit(solution)/shard_map/all_gather | solution.py:10
  84.9 0.0 copy-start.1
  84.9 6.8 convolution_bitcast_fusion
  91.7 0.0 all-reduce.9.cloned.1.call-update
  91.8 0.0 reduce-scatter.2.cloned.1.call-start
  91.8 0.0 all-to-all-done
  91.8 0.4 reshape.14
  92.2 0.0 copy-done.1
  92.2 6.3 multiply_reduce_fusion
  98.5 0.0 copy-start
  98.5 0.0 reduce-scatter.2.cloned.1.call-update
  98.6 0.0 all-reduce.5.cloned.1.call-start
  98.6 0.4 reshape.13
  99.0 1.7 fusion.9
  100.7 0.0 all-reduce.5.cloned.1.call-update
  100.7 0.4 fusion.10
  101.2 1.3 dynamic-slice
  103.1 106.0 %psum.23 = f32[8,256]{1,0:T(8,128)S(1)} all-reduce(f32[8,256]{1,0:T(8,128)S(1)} %get-tuple-element.3), channel_id=1, replica_groups=mesh['row'=64,'col'=8] {'row','col'}, use_global_device_ids=true, to_apply=%region_6.0 | all-reduce | flops 2048 | bytes 16384 | tf_op jit(solution)/shard_map/psum | solution.py:25
  209.1 302.3 %all-reduce.7.cloned.1.call-done = f32[256,256]{1,0:T(8,128)} async-done(((f32[256,256]{1,0:T(8,128)}), f32[256,256]{1,0:T(8,128)}) %all-reduce.7.cloned.1.call-update) | async-done | bytes 262160 | tf_op jit(solution)/shard_map/psum | solution.py:27
  511.4 846.1 %all-reduce.9.cloned.1.call-done = f32[256,1024]{1,0:T(8,128)} async-done(((f32[256,1024]{1,0:T(8,128)}), f32[256,1024]{1,0:T(8,128)}) %all-reduce.9.cloned.1.call-update) | async-done | bytes 1048592
  1357.5 2.0 convolution_subtract_fusion
  1359.5 0.0 reduce-scatter.2.cloned.1.call-done
  1359.5 88.9 %all-reduce.5.cloned.1.call-done = f32[256,256]{1,0:T(8,128)} async-done(((f32[256,256]{1,0:T(8,128)}), f32[256,256]{1,0:T(8,128)}) %all-reduce.5.cloned.1.call-update) | async-done | bytes 262160 | tf_op jit(solution)/shard_map/psum | solution.py:28
  1448.4 0.0 copy-done
  1448.4 1.8 fusion
  1450.2 1.9 fusion.1
Async XLA Ops:
  10.0 81.9 %all-to-all-start = ((f32[64,4,1024]{2,1,0:T(4,128)}), f32[64,4,1024]{2,1,0:T(4,128)S(1)}, u32[]{:S(2)}, u32[]{:S(2)}) async-start(f32[64,4,1024]{2,1,0:T(4,128)} %stack.2), calls=%async_computation | async-start | bytes 2097152 | tf_op jit(solution)/shard_map/all_to_all | solution.py:14
  31.2 480.2 %all-reduce.7.cloned.1.call-start = ((), (), s32[]{:S(2)}) async-start(), calls=%async_computation.4 | async-start | bytes 524288 | tf_op jit(solution)/shard_map/psum | solution.py:27
  33.2 1324.3 %all-reduce.9.cloned.1.call-start = ((), (), s32[]{:S(2)}) async-start(), calls=%async_computation.5 | async-start | bytes 2097152
  84.9 7.3 copy-start.1
  91.8 1267.7 %reduce-scatter.2.cloned.1.call-start = ((), (), s32[]{:S(2)}) async-start(), calls=%async_computation.3 | async-start | bytes 147456 | tf_op jit(solution)/shard_map/reduce_scatter | solution.py:24
  98.5 1349.9 %copy-start = (f32[16,256]{1,0:T(8,128)S(1)}, f32[16,256]{1,0:T(8,128)}, u32[]{:S(2)}) copy-start(f32[16,256]{1,0:T(8,128)} %param.5) | copy-start | bytes 49156
  98.6 1349.8 %all-reduce.5.cloned.1.call-start = ((), (), s32[]{:S(2)}) async-start(), calls=%async_computation.2 | async-start | bytes 524288 | tf_op jit(solution)/shard_map/psum | solution.py:28
Sparse Core Ops, SparseCore 0:
  37.5 473.8 all-reduce.6
  514.3 843.1 all-reduce.8
  1360.4 87.9 all-reduce.4
Sparse Core Ops, SparseCore 1:
  98.7 42.0 reduce-scatter.1

commit v3 on v0

--- a/solution.py
+++ b/solution.py
@@ -24,7 +24,9 @@
     mttkrp_c = lax.psum(partial_c, ("row", "col"))
     local_gram_a = jnp.dot(factor_a.T, factor_a, precision=highest)
     gram_a = lax.psum(local_gram_a, ("row", "col"))
-    gram_b = lax.psum(jnp.dot(block_bt, block_bt.T, precision=highest), "col")
+    own = jnp.dot(block_bt, block_bt.T, precision=highest)
+    terms = lax.all_gather(own, "col", axis=0, tiled=False)
+    gram_b = terms.sum(axis=0)
     grad_a = jnp.dot(factor_a, gram_b * gram_c, precision=highest) - mttkrp_a
     h_rows = lax.dynamic_slice_in_dim(
         gram_a * gram_c, lax.axis_index("row") * rank_rows, rank_rows, 0

time: 1440 us -> 1360 us (0.944)
  the two profiles are of different devices: /device:TPU:2 before, /device:TPU:8 now
where the time goes in v3:
time: 1360 us
  waiting for transfers between devices  1200 us (88%)
  blocking collectives  116 us (9%)
  matrix products  21.6 us (2%)
  between operations  15.9 us (1%)
    unnamed x6, waiting for transfers between devices  852 us
    psum x1, waiting for transfers between devices, local(): gram_a = lax.psum(local_gram_a, ('row', 'col'))  257 us
    psum x1, blocking collectives, local(): mttkrp_c = lax.psum(partial_c, ('row', 'col'))  101 us
    all_gather x1, waiting for transfers between devices, local(): block_bt = lax.all_gather(factor_bt, 'row', axis=0, tiled=True)  89.4 us
  transfers between devices with their start and end apart: 5, of which 3 were waited for; matrix products, arithmetic and copies ran while one was open for 2% of the time, Pallas kernels for 0%

profile of v3, /device:TPU:8, one launch (start us, length us, event | category | flops | bytes accessed | tf_op | source)
XLA Modules:
  0.0 1357.0 jit_solution(2287250758616800934)
XLA Ops:
  8.0 0.0 all-gather.7.cloned.1.call-start
  8.0 0.7 all-gather.7.cloned.1.call-update
  8.7 0.0 all-reduce.4.cloned.1.call-start
  8.8 1.9 fusion.11
  10.7 0.0 all-reduce.4.cloned.1.call-update
  10.7 0.0 all-reduce.6.cloned.1.call-start
  10.8 15.1 %all_gather.15 = f32[128,256]{1,0:T(8,128)S(1)} all-gather(f32[16,256]{1,0:T(8,128)} %param.5), channel_id=1, replica_groups=mesh['row'=64,'col'=8] {'col'}, dimensions={0}, use_global_device_ids=true | all-gather | bytes 147456 | tf_op jit(solution)/shard_map/all_gather | solution.py:10
  25.9 6.7 convolution_bitcast_fusion
  32.6 0.0 all-reduce.6.cloned.1.call-update
  32.6 0.0 all-gather.5.cloned.1.call-start
  32.7 89.4 %all-gather.7.cloned.1.call-done = f32[64,4,1024]{2,1,0:T(4,128)} async-done(((f32[1,4,1024]{2,1,0:T(4,128)}), f32[64,4,1024]{2,1,0:T(4,128)}) %all-gather.7.cloned.1.call-update) | async-done | bytes 1048592 | tf_op jit(solution)/shard_map/all_gather | solution.py:13
  122.1 1.7 reshape.10
  123.8 1.7 fusion.9
  125.5 0.0 all-gather.5.cloned.1.call-update
  125.6 0.0 reduce-scatter.2.cloned.1.call-start
  125.6 0.0 copy-done
  125.6 0.4 reshape.11
  126.0 0.0 copy-done.3
  126.0 0.0 copy-start.2
  126.0 6.3 multiply_reduce_fusion
  132.4 0.0 reduce-scatter.2.cloned.1.call-update
  132.4 0.4 fusion.10
  132.8 1.3 dynamic-slice
  134.8 100.7 %psum.15 = f32[8,256]{1,0:T(8,128)S(1)} all-reduce(f32[8,256]{1,0:T(8,128)S(1)} %get-tuple-element.3), channel_id=1, replica_groups=mesh['row'=64,'col'=8] {'row','col'}, use_global_device_ids=true, to_apply=%region_6.0 | all-reduce | flops 2048 | bytes 16384 | tf_op jit(solution)/shard_map/psum | solution.py:24
  235.4 256.6 %all-reduce.4.cloned.1.call-done = f32[256,256]{1,0:T(8,128)} async-done(((f32[256,256]{1,0:T(8,128)}), f32[256,256]{1,0:T(8,128)}) %all-reduce.4.cloned.1.call-update) | async-done | bytes 262160 | tf_op jit(solution)/shard_map/psum | solution.py:26
  492.0 851.6 %all-reduce.6.cloned.1.call-done = f32[256,1024]{1,0:T(8,128)} async-done(((f32[256,1024]{1,0:T(8,128)}), f32[256,1024]{1,0:T(8,128)}) %all-reduce.6.cloned.1.call-update) | async-done | bytes 1048592
  1343.6 2.0 convolution_subtract_fusion
  1345.6 1.8 reduce_sum.27
  1347.4 0.0 reduce-scatter.2.cloned.1.call-done
  1347.4 0.0 copy-done.2
  1347.4 1.6 fusion
  1349.0 0.9 fusion.1
  (5 shorter events, 0.0 us)
Async XLA Ops:
  8.0 114.1 %all-gather.7.cloned.1.call-start = ((), (), s32[]{:S(2)}) async-start(), calls=%async_computation.4 | async-start | bytes 1064960 | tf_op jit(solution)/shard_map/all_gather | solution.py:13
  8.7 483.3 %all-reduce.4.cloned.1.call-start = ((), (), s32[]{:S(2)}) async-start(), calls=%async_computation.2 | async-start | bytes 524288 | tf_op jit(solution)/shard_map/psum | solution.py:26
  10.7 1332.9 %all-reduce.6.cloned.1.call-start = ((), (), s32[]{:S(2)}) async-start(), calls=%async_computation.5 | async-start | bytes 2097152
  32.6 93.4 %copy-start.3 = (f32[8,256]{1,0:T(8,128)S(1)}, f32[8,256]{1,0:T(8,128)}, u32[]{:S(2)}) copy-start(f32[8,256]{1,0:T(8,128)} %param.7) | copy-start | bytes 24580
  32.6 1313.0 %all-gather.5.cloned.1.call-start = ((), (), s32[]{:S(2)}) async-start(), calls=%async_computation.3 | async-start | bytes 2359296 | tf_op jit(solution)/shard_map/all_gather | solution.py:28
  122.1 3.5 copy-start
  125.6 1221.8 %reduce-scatter.2.cloned.1.call-start = ((), (), s32[]{:S(2)}) async-start(), calls=%async_computation.1 | async-start | bytes 147456 | tf_op jit(solution)/shard_map/reduce_scatter | solution.py:23
  126.0 1221.4 %copy-start.2 = (f32[16,256]{1,0:T(8,128)S(1)}, f32[16,256]{1,0:T(8,128)}, u32[]{:S(2)}) copy-start(f32[16,256]{1,0:T(8,128)} %param.5) | copy-start | bytes 49156
  492.0 857.0 %copy-start.1 = (f32[256,256]{1,0:T(8,128)S(1)}, f32[256,256]{1,0:T(8,128)}, u32[]{:S(2)}) copy-start(f32[256,256]{1,0:T(8,128)} %all-reduce.4.cloned.1.call-done) | copy-start | bytes 786436
Sparse Core Ops, SparseCore 0:
  13.0 109.0 all-gather.6
  125.7 38.3 all-gather.4
  166.8 40.8 reduce-scatter.1
Sparse Core Ops, SparseCore 1:
  14.7 477.3 all-reduce.3
  494.8 848.8 all-reduce.5
